TPU v7x, 256 devices: a whole 4x4x8 slice. The times are simulated.
256 devices in a mesh: dp: 8 (over z), row: 8 (over y_hi, x), col: 4 (over y_lo, core).
Axes of the slice: x: 4, y: 4 (y_hi: 2, y_lo: 2; y = y_hi * 2 + y_lo), z: 8, core: 2. Of those that a mesh axis runs over, the one named last changes fastest.
Arguments:
- inputs: bfloat16 [8, 192, 64, 512], P('dp', None, 'row', 'col'), may hold values from -16 to 16
- norm_gain: float32 [192], replicated, may hold values from 0.25 to 1.75
- w_expand: bfloat16 [192, 768], replicated, may hold values from -0.4375 to 0.4375
- kernel: float32 [768, 9], replicated, may hold values from -2 to 2
- w_squeeze: float32 [768, 48], replicated, may hold values from -1.5 to 1.5
- w_excite: float32 [48, 768], replicated, may hold values from -6 to 6
- w_project: bfloat16 [768, 192], replicated, may hold values from -0.21875 to 0.21875
- cotangent: bfloat16 [8, 192, 64, 512], P('dp', None, 'row', 'col'), may hold values from -16 to 16
Outputs:
- output: bfloat16 [8, 192, 64, 512], P('dp', None, 'row', 'col')
- grad_inputs: bfloat16 [8, 192, 64, 512], P('dp', None, 'row', 'col')
- grad_gain: float32 [192], replicated
- grad_w_expand: float32 [192, 768], replicated
- grad_kernel: float32 [768, 9], replicated
- grad_w_squeeze: float32 [768, 48], replicated
- grad_w_excite: float32 [48, 768], replicated
- grad_w_project: float32 [768, 192], replicated
All inputs are finite; a program needn't handle non-finite values.
Results may differ from a plain program's by a relative error of at most 0.0019.
Values may be sent and summed in bfloat16 or wider, within the bound.
No kernel may reach another device: no remote copies, remote signals or barrier semaphores. Data moves between devices by JAX's collectives and lax.ppermute only.
A program may use at most 64 MiB of HBM per device.

v0:
```python
import jax
import jax.numpy as jnp
from jax import lax
from jax.sharding import PartitionSpec as P

EPS = 1e-06
HIGH = lax.Precision.HIGHEST


def with_halo(shard, sides, width):
    for axis, dim in sides:
        count, length = (lax.axis_size(axis), shard.shape[dim])
        up = [(i, (i + 1) % count) for i in range(count - 1)]
        down = [(j, i) for i, j in up]
        last = lax.slice_in_dim(shard, length - width, length, axis=dim)
        leading = lax.slice_in_dim(shard, 0, width, axis=dim)
        before = lax.ppermute(last, axis, up)
        after = lax.ppermute(leading, axis, down)
        shard = jnp.concatenate([before, shard, after], axis=dim)
    return shard


def silu_slope(value):
    sig = jax.nn.sigmoid(value)
    return sig * (1.0 + value * (1.0 - sig))


def normalize(inputs, norm_gain):
    widened = inputs.astype(jnp.float32)
    inverse = lax.rsqrt(jnp.mean(widened * widened, axis=1, keepdims=True) + EPS)
    normed = widened * inverse
    scaled = (normed * norm_gain[None, :, None, None]).astype(jnp.bfloat16)
    return (normed, inverse, scaled)


def expand(scaled, w_expand):
    return jnp.einsum("bchw,ce->behw", scaled, w_expand, preferred_element_type=jnp.float32)


def depthwise(hidden_pad, kernel, out_rows, out_cols):
    total = jnp.zeros((hidden_pad.shape[0], hidden_pad.shape[1], out_rows, out_cols), jnp.float32)
    for tap in range(9):
        drow, dcol = (tap // 3, tap % 3)
        total = (
            total
            + kernel[:, tap][None, :, None, None]
            * hidden_pad[:, :, drow : drow + out_rows, dcol : dcol + out_cols]
        )
    return total


def local(inputs, norm_gain, w_expand, kernel, w_squeeze, w_excite, w_project, cotangent):
    batch, chans, rows, cols = inputs.shape
    pixels = rows * cols * lax.axis_size("row") * lax.axis_size("col")
    normed, inverse, scaled = normalize(inputs, norm_gain)
    pre = expand(scaled, w_expand)
    hidden = jax.nn.silu(pre).astype(jnp.bfloat16)
    hidden_pad = with_halo(hidden, (("row", 2), ("col", 3)), 1)
    conv = depthwise(hidden_pad, kernel, rows, cols)
    act = jax.nn.silu(conv)
    pooled = lax.psum(jnp.sum(act, axis=(2, 3)), ("row", "col")) / pixels
    squeeze_pre = jnp.dot(pooled, w_squeeze, precision=HIGH)
    squeezed = jax.nn.silu(squeeze_pre)
    excite_pre = jnp.dot(squeezed, w_excite, precision=HIGH)
    excite = jax.nn.sigmoid(excite_pre)
    gated = (act * excite[:, :, None, None]).astype(jnp.bfloat16)
    proj = jnp.einsum("behw,ec->bchw", gated, w_project, preferred_element_type=jnp.float32)
    output = (inputs.astype(jnp.float32) + proj).astype(jnp.bfloat16)
    grad_gated = jnp.einsum(
        "bchw,ec->behw", cotangent, w_project, preferred_element_type=jnp.float32
    )
    grad_project = jnp.einsum("behw,bchw->ec", gated, cotangent, preferred_element_type=jnp.float32)
    grad_excite = lax.psum(jnp.sum(grad_gated * act, axis=(2, 3)), ("row", "col"))
    grad_epre = grad_excite * excite * (1.0 - excite)
    grad_wexc = jnp.einsum("bs,be->se", squeezed, grad_epre, precision=HIGH)
    grad_spre = jnp.einsum("be,se->bs", grad_epre, w_excite, precision=HIGH) * silu_slope(
        squeeze_pre
    )
    grad_wsq = jnp.einsum("be,bs->es", pooled, grad_spre, precision=HIGH)
    grad_pooled = jnp.einsum("bs,es->be", grad_spre, w_squeeze, precision=HIGH)
    grad_act = grad_gated * excite[:, :, None, None] + (grad_pooled / pixels)[:, :, None, None]
    grad_conv = (grad_act * silu_slope(conv)).astype(jnp.bfloat16)
    grad_pad = with_halo(grad_conv, (("row", 2), ("col", 3)), 1)
    grad_hidden = jnp.zeros(pre.shape, jnp.float32)
    taps = []
    for tap in range(9):
        drow, dcol = (tap // 3, tap % 3)
        grad_hidden = (
            grad_hidden
            + kernel[:, tap][None, :, None, None]
            * grad_pad[:, :, 2 - drow : 2 - drow + rows, 2 - dcol : 2 - dcol + cols]
        )
        taps.append(
            jnp.sum(
                grad_conv.astype(jnp.float32)
                * hidden_pad[:, :, drow : drow + rows, dcol : dcol + cols].astype(jnp.float32),
                axis=(0, 2, 3),
            )
        )
    grad_kernel = jnp.stack(taps, axis=1)
    grad_pre = (grad_hidden * silu_slope(pre)).astype(jnp.bfloat16)
    grad_wexp = jnp.einsum("bchw,behw->ce", scaled, grad_pre, preferred_element_type=jnp.float32)
    grad_scaled = jnp.einsum(
        "ce,behw->bchw", w_expand, grad_pre, preferred_element_type=jnp.float32
    )
    grad_gain = jnp.sum(grad_scaled * normed, axis=(0, 2, 3))
    grad_normed = grad_scaled * norm_gain[None, :, None, None]
    grad_in = inverse * (
        grad_normed - normed * jnp.mean(grad_normed * normed, axis=1, keepdims=True)
    ) + cotangent.astype(jnp.float32)
    grad_wsq_all, grad_wexc_all = lax.psum((grad_wsq, grad_wexc), "dp")
    gain_all, wexp_all, kernel_all, project_all = lax.psum(
        (grad_gain, grad_wexp, grad_kernel, grad_project), ("dp", "row", "col")
    )
    return (
        output,
        grad_in.astype(jnp.bfloat16),
        gain_all,
        wexp_all,
        kernel_all,
        grad_wsq_all,
        grad_wexc_all,
        project_all,
    )


def solution(mesh):
    placed = (
        P("dp", None, "row", "col"),
        P(),
        P(),
        P(),
        P(),
        P(),
        P(),
        P("dp", None, "row", "col"),
    )
    return jax.shard_map(
        local,
        mesh=mesh,
        in_specs=placed,
        out_specs=(
            P("dp", None, "row", "col"),
            P("dp", None, "row", "col"),
            P(),
            P(),
            P(),
            P(),
            P(),
            P(),
        ),
        check_vma=False,
    )
```

profile of v0, /device:TPU:2, one launch (start us, length us, event | category | flops | bytes accessed | tf_op | source)
XLA Modules:
  0.0 487.3 jit_solution(15300703473995289829)
XLA Ops:
  7.2 1.1 fusion.59
  8.4 3.8 fusion.30
  12.2 3.4 collective-permute-start
  15.6 2.5 collective-permute-start.1
  18.1 2.7 collective-permute-done
  20.7 3.1 collective-permute-done.1
  23.9 1.3 collective-permute-start.2
  25.2 1.4 collective-permute-start.3
  26.8 3.5 collective-permute-done.3
  31.3 7.2 %fusion.26 = (f32[768]{0:T(1024)S(1)}, f32[768]{0:T(1024)S(1)}, f32[1,768,8,128]{1,3,2,0:T(8,128)}, f32[768,8,128]{0,2,1:T(8,128)}) fusion(bf16[1,768,10,129]{1,3,2,0:T(8,128)(2,1)S(1)} %get-tuple-element.60, f32[768]{0:T(1024)S(1)} %get-tuple-element.41, bf16[1,768,1,128]{1,3,2,0:T(8,128)(2,1)S(1)} %collective-permute-done.1, ...), kind=kOutput, calls=%fused_computation.48 | convolution fusion | flops 329513472 | bytes 19989504 | tf_op jit(solution)/shard_map/bchw,ec->behw/dot_general | solution.py:69
  38.5 57.0 %all-reduce.2 = (f32[1,768]{1,0:T(1,128)S(1)}, f32[1,768]{1,0:T(1,128)S(1)}) all-reduce(f32[1,768]{1,0:T(1,128)S(1)} %reduce_sum.132, f32[1,768]{1,0:T(1,128)S(1)} %reduce_sum.134), channel_id=1, replica_groups=mesh['dp'=8,'row'=8,'col'=4] {'row','col'}, use_global_device_ids=true, to_apply=%region_2.3 | all-reduce | flops 1536 | bytes 12288 | tf_op jit(solution)/shard_map/psum | solution.py:61
  96.1 3.9 fusion.46
  100.0 1.9 convolution_bitcast_fusion.1
  103.4 5.6 %fusion.24 = (f32[768]{0:T(1024)S(1)}, f32[768]{0:T(1024)S(1)}, f32[768]{0:T(1024)S(1)}, f32[768]{0:T(1024)S(1)}, f32[768]{0:T(1024)S(1)}, /*index=5*/f32[768]{0...) fusion(bf16[1,768,10,129]{1,3,2,0:T(8,128)(2,1)S(1)} %copy-done.4, ...), kind=kLoop, calls=%fused_computation.44 | loop fusion | flops 32236800 | bytes 20874240 | tf_op jit(solution)/shard_map/reduce_sum | solution.py:94
  109.0 2.1 collective-permute-start.4
  111.1 11.1 %collective-permute-start.5 = (bf16[1,768,1,128]{1,3,2,0:T(8,128)(2,1)S(1)}, bf16[1,768,1,128]{1,3,2,0:T(8,128)(2,1)S(1)}, u32[]{:S(2)}, u32[]{:S(2)}) collective-permute-start(bf16[1,768,1,128]{1,3,2,0:T(8,128)(2,1)S(1)} %get-tuple-element.64), channel_id=1, source_target_pairs={{4,0},{8,4},{12,8},{16,12},{20,16},{24,20},{28,24},{5,1},{9,5},{13... | collective-permute-start | bytes 589832 | tf_op jit(solution)/shard_map/ppermute | solution.py:18
  122.9 1.0 collective-permute-done.4
  123.8 1.5 collective-permute-done.5
  125.4 1.3 collective-permute-start.6
  126.7 3.0 collective-permute-start.7
  130.5 1.0 copy.24
  133.8 4.7 fusion.15
  138.5 1.1 copy-done.12
  139.7 1.4 fusion.43
  141.1 2.2 fusion.58
  143.5 1.0 copy.25
  144.5 81.3 %all-reduce = (f32[192]{0:T(256)}, f32[768,9]{0,1:T(8,128)}) all-reduce(f32[192]{0:T(256)S(1)} %get-tuple-element.32, f32[768,9]{0,1:T(8,128)S(1)} %stack.39), channel_id=1, replica_groups=mesh['dp'=8,'row'=8,'col'=4] {'dp','row','col'}, use_global_device_ids=true, to_apply=%region_7.8 | all-reduce | flops 7104 | bytes 56832 | tf_op jit(solution)/shard_map/psum | solution.py:112
  225.8 247.7 %all-reduce.7.cloned.1.call-done = (f32[192,768]{1,0:T(8,128)}, f32[768,192]{0,1:T(8,128)}) async-done(((f32[192,768]{1,0:T(8,128)}, f32[768,192]{0,1:T(8,128)}), (f32[192,768]{1,0:T(8,128)}, f32[768,192]{0,1:T(8,128)})) %all-reduce.7.cloned.1.call-update) | async-done | bytes 1179664 | tf_op jit(solution)/shard_map/psum | solution.py:112
  473.5 1.9 copy.51
  475.4 1.6 copy.52
  477.0 1.6 copy.53
  478.6 1.9 copy.54
  (84 shorter events, 7.0 us)
Async XLA Ops:
  7.2 24.1 %copy-start = (bf16[768,192]{0,1:T(8,128)(2,1)S(1)}, bf16[768,192]{0,1:T(8,128)(2,1)}, u32[]{:S(2)}) copy-start(bf16[768,192]{0,1:T(8,128)(2,1)} %param.14) | copy-start | bytes 884740
  7.2 218.6 %all-reduce.9.cloned.1.call-start = ((), (), s32[]{:S(2)}) async-start(), calls=%async_computation.1 | async-start | bytes 589824 | tf_op jit(solution)/shard_map/psum | solution.py:111
  8.4 18.3 %copy-start.20 = (f32[768,9]{0,1:T(8,128)S(1)}, f32[768,9]{0,1:T(8,128)}, u32[]{:S(2)}) copy-start(f32[768,9]{0,1:T(8,128)} %param.11) | copy-start | bytes 82948
  12.2 8.5 %collective-permute-start = (bf16[1,768,1,128]{1,3,2,0:T(8,128)(2,1)S(1)}, bf16[1,768,1,128]{1,3,2,0:T(8,128)(2,1)S(1)}, u32[]{:S(2)}, u32[]{:S(2)}) collective-permute-start(bf16[1,768,1,128]{1,3,2,0:T(8,128)(2,1)S(1)} %get-tuple-element.65), channel_id=1, source_target_pairs={{0,4},{4,8},{8,12},{12,16},{16,20},{20,24},{24,28},{1,5},{5,9},{9,... | collective-permute-start | bytes 589832 | tf_op jit(solution)/shard_map/ppermute | solution.py:17
  15.6 8.3 %collective-permute-start.1 = (bf16[1,768,1,128]{1,3,2,0:T(8,128)(2,1)S(1)}, bf16[1,768,1,128]{1,3,2,0:T(8,128)(2,1)S(1)}, u32[]{:S(2)}, u32[]{:S(2)}) collective-permute-start(bf16[1,768,1,128]{1,3,2,0:T(8,128)(2,1)S(1)} %get-tuple-element.66), channel_id=1, source_target_pairs={{4,0},{8,4},{12,8},{16,12},{20,16},{24,20},{28,24},{5,1},{9,5},{13... | collective-permute-start | bytes 589832 | tf_op jit(solution)/shard_map/ppermute | solution.py:18
  20.7 10.5 %copy-start.8 = (bf16[1,768,1,128]{1,3,2,0:T(8,128)(2,1)}, bf16[1,768,1,128]{1,3,2,0:T(8,128)(2,1)S(1)}, u32[]{:S(2)}) copy-start(bf16[1,768,1,128]{1,3,2,0:T(8,128)(2,1)S(1)} %collective-permute-done) | copy-start | bytes 589828
  23.9 7.3 %copy-start.10 = (bf16[1,768,1,128]{1,3,2,0:T(8,128)(2,1)}, bf16[1,768,1,128]{1,3,2,0:T(8,128)(2,1)S(1)}, u32[]{:S(2)}) copy-start(bf16[1,768,1,128]{1,3,2,0:T(8,128)(2,1)S(1)} %collective-permute-done.1) | copy-start | bytes 589828
  23.9 2.8 collective-permute-start.2
  25.2 6.0 %copy-start.17 = (bf16[1,192,8,128]{3,2,1,0:T(8,128)(2,1)S(1)}, bf16[1,192,8,128]{3,2,1,0:T(8,128)(2,1)}, u32[]{:S(2)}) copy-start(bf16[1,192,8,128]{3,2,1,0:T(8,128)(2,1)} %param.15) | copy-start | bytes 1179652
  25.2 5.0 %collective-permute-start.3 = (bf16[1,768,10,1]{1,3,2,0:T(2,128)(2,1)S(1)}, bf16[1,768,10,1]{1,3,2,0:T(2,128)(2,1)S(1)}, u32[]{:S(2)}, u32[]{:S(2)}) collective-permute-start(bf16[1,768,10,1]{1,3,2,0:T(2,128)(2,1)S(1)} %get-tuple-element.62), channel_id=1, source_target_pairs={{1,0},{2,1},{3,2},{5,4},{6,5},{7,6},{9,8},{10,9},{11,10},{13,12},{... | collective-permute-start | bytes 46088 | tf_op jit(solution)/shard_map/ppermute | solution.py:18
  31.2 7.3 %copy-start.1 = (bf16[1,768,10,129]{1,3,2,0:T(8,128)(2,1)}, bf16[1,768,10,129]{1,3,2,0:T(8,128)(2,1)S(1)}, u32[]{:S(2)}) copy-start(bf16[1,768,10,129]{1,3,2,0:T(8,128)(2,1)S(1)} %get-tuple-element.59) | copy-start | bytes 5944324
  31.2 7.3 %copy-start.3 = (bf16[1,768,10,129]{1,3,2,0:T(8,128)(2,1)}, bf16[1,768,10,129]{1,3,2,0:T(8,128)(2,1)S(1)}, u32[]{:S(2)}) copy-start(bf16[1,768,10,129]{1,3,2,0:T(8,128)(2,1)S(1)} %get-tuple-element.60) | copy-start | bytes 5944324
  31.2 64.3 %copy-start.16 = (f32[768,48]{0,1:T(8,128)S(1)}, f32[768,48]{0,1:T(8,128)}, u32[]{:S(2)}) copy-start(f32[768,48]{0,1:T(8,128)} %param.12) | copy-start | bytes 442372
  31.3 64.5 %copy-start.15 = (f32[48,768]{1,0:T(8,128)S(1)}, f32[48,768]{1,0:T(8,128)}, u32[]{:S(2)}) copy-start(f32[48,768]{1,0:T(8,128)} %param.13) | copy-start | bytes 442372
  31.3 64.8 %copy-start.13 = (bf16[1,192,8,128]{3,2,1,0:T(8,128)(2,1)S(1)}, bf16[1,192,8,128]{3,2,1,0:T(8,128)(2,1)}, u32[]{:S(2)}) copy-start(bf16[1,192,8,128]{3,2,1,0:T(8,128)(2,1)} %param.8) | copy-start | bytes 1179652
  96.1 3.9 copy-start.6
  100.0 2.5 copy-start.2
  100.0 2.5 copy-start.4
  100.0 3.4 copy-start.7
  100.0 3.4 copy-start.9
  100.0 3.4 copy-start.11
  109.0 21.6 %copy-start.19 = (bf16[1,192,8,128]{3,1,2,0:T(8,128)(2,1)S(1)}, bf16[1,192,8,128]{3,1,2,0:T(8,128)(2,1)}, u32[]{:S(2)}) copy-start(bf16[1,192,8,128]{3,1,2,0:T(8,128)(2,1)} %fusion.46) | copy-start | bytes 1179652
  109.0 14.8 %collective-permute-start.4 = (bf16[1,768,1,128]{1,3,2,0:T(8,128)(2,1)S(1)}, bf16[1,768,1,128]{1,3,2,0:T(8,128)(2,1)S(1)}, u32[]{:S(2)}, u32[]{:S(2)}) collective-permute-start(bf16[1,768,1,128]{1,3,2,0:T(8,128)(2,1)S(1)} %get-tuple-element.63), channel_id=1, source_target_pairs={{0,4},{4,8},{8,12},{12,16},{16,20},{20,24},{24,28},{1,5},{5,9},{9,... | collective-permute-start | bytes 589832 | tf_op jit(solution)/shard_map/ppermute | solution.py:17
  111.1 14.2 %collective-permute-start.5 = (bf16[1,768,1,128]{1,3,2,0:T(8,128)(2,1)S(1)}, bf16[1,768,1,128]{1,3,2,0:T(8,128)(2,1)S(1)}, u32[]{:S(2)}, u32[]{:S(2)}) collective-permute-start(bf16[1,768,1,128]{1,3,2,0:T(8,128)(2,1)S(1)} %get-tuple-element.64), channel_id=1, source_target_pairs={{4,0},{8,4},{12,8},{16,12},{20,16},{24,20},{28,24},{5,1},{9,5},{13... | collective-permute-start | bytes 589832 | tf_op jit(solution)/shard_map/ppermute | solution.py:18
  125.4 6.5 %collective-permute-start.6 = (bf16[1,768,10,1]{1,3,2,0:T(2,128)(2,1)S(1)}, bf16[1,768,10,1]{1,3,2,0:T(2,128)(2,1)S(1)}, u32[]{:S(2)}, u32[]{:S(2)}) collective-permute-start(bf16[1,768,10,1]{1,3,2,0:T(2,128)(2,1)S(1)} %get-tuple-element.57), channel_id=1, source_target_pairs={{1,0},{2,1},{3,2},{5,4},{6,5},{7,6},{9,8},{10,9},{11,10},{13,12},{... | collective-permute-start | bytes 46088 | tf_op jit(solution)/shard_map/ppermute | solution.py:18
  126.7 5.2 %collective-permute-start.7 = (bf16[1,768,10,1]{1,3,2,0:T(2,128)(2,1)S(1)}, bf16[1,768,10,1]{1,3,2,0:T(2,128)(2,1)S(1)}, u32[]{:S(2)}, u32[]{:S(2)}) collective-permute-start(bf16[1,768,10,1]{1,3,2,0:T(2,128)(2,1)S(1)} %get-tuple-element.58), channel_id=1, source_target_pairs={{0,1},{1,2},{2,3},{4,5},{5,6},{6,7},{8,9},{9,10},{10,11},{12,13},{... | collective-permute-start | bytes 46088 | tf_op jit(solution)/shard_map/ppermute | solution.py:17
  131.6 341.9 %all-reduce.7.cloned.1.call-start = ((), (), s32[]{:S(2)}) async-start(), calls=%async_computation | async-start | bytes 2359296 | tf_op jit(solution)/shard_map/psum | solution.py:112
  131.9 1.9 copy-start.5
  133.8 5.9 %copy-start.14 = (bf16[1,192,8,128]{3,2,1,0:T(8,128)(2,1)S(1)}, bf16[1,192,8,128]{3,2,1,0:T(8,128)(2,1)}, u32[]{:S(2)}) copy-start(bf16[1,192,8,128]{3,2,1,0:T(8,128)(2,1)} %param.8) | copy-start | bytes 1179652
  133.8 5.9 %copy-start.21 = (f32[192]{0:T(256)S(1)}, f32[192]{0:T(256)}, u32[]{:S(2)}) copy-start(f32[192]{0:T(256)} %param.9) | copy-start | bytes 2308
  139.7 1.4 copy-start.22
  139.7 3.6 copy-start.18
  (1 other events, 1.2 us)
Sparse Core Ops, SparseCore 0:
  131.7 75.7 all-reduce.8
  213.6 259.8 all-reduce.6
where the time goes:
time: 488 us; the launch traced here: 487 us
  waiting for transfers between devices  259 us (53%)
  blocking collectives  138 us (28%)
  starting transfers between devices  26.3 us (5%)
  matrix products  21.3 us (4%)
  other arithmetic  15.1 us (3%)
  between operations  14.5 us (3%)
  local copies, waits for them, and re-layouts  12.4 us (3%)
    psum x1, waiting for transfers between devices, local(): lax.psum((grad_gain, grad_wexp, grad_kernel, grad_project), ('dp', 'row',...  248 us
    psum x1, blocking collectives, local(): lax.psum((grad_gain, grad_wexp, grad_kernel, grad_project), ('dp', 'row',...  81.3 us
    psum x1, blocking collectives, local(): pooled = lax.psum(jnp.sum(act, axis=(2, 3)), ('row', 'col')) / pixels  57 us
    ppermute x4, starting transfers between devices, with_halo(): after = lax.ppermute(leading, axis, down)  16.2 us
    unnamed x52, local copies, waits for them, and re-layouts  12.1 us
    ppermute x4, starting transfers between devices, with_halo(): before = lax.ppermute(last, axis, up)  9.77 us
  transfers between devices with their start and end apart: 10, of which 6 were waited for; matrix products, arithmetic and copies ran while one was open for 3% of the time, Pallas kernels for 0%

commit v1 on v0

--- a/solution.py
+++ b/solution.py
@@ -58,7 +58,7 @@
     hidden_pad = with_halo(hidden, (("row", 2), ("col", 3)), 1)
     conv = depthwise(hidden_pad, kernel, rows, cols)
     act = jax.nn.silu(conv)
-    pooled = lax.psum(jnp.sum(act, axis=(2, 3)), ("row", "col")) / pixels
+    pooled = jnp.sum(lax.all_gather(jnp.sum(act, axis=(2, 3)), ("row", "col")), axis=0) / pixels
     squeeze_pre = jnp.dot(pooled, w_squeeze, precision=HIGH)
     squeezed = jax.nn.silu(squeeze_pre)
     excite_pre = jnp.dot(squeezed, w_excite, precision=HIGH)

time: 488 us -> 527 us (1.080)
  blocking collectives: 138 us -> 173 us
    all_gather x0 -> x1, blocking collectives: none -> 36.3 us  [local(): lax.all_gather(jnp.sum(act, axis=(2, 3)), ('row', 'col'))]
    unnamed x52 -> x43, local copies, waits for them, and re-layouts: 12.1 us -> 11.2 us
  transfers between devices with their start and end apart: 10 -> 10, of which waited for: 6 -> 6; matrix products, arithmetic and copies ran while one was open for 3% -> 2% of each run, Pallas kernels for 0% -> 0%
where the time goes in v1:
time: 527 us
  waiting for transfers between devices  262 us (50%)
  blocking collectives  173 us (33%)
  starting transfers between devices  26.2 us (5%)
  matrix products  21.3 us (4%)
  other arithmetic  18.9 us (4%)
  between operations  14.5 us (3%)
  local copies, waits for them, and re-layouts  11.5 us (2%)
    psum x1, waiting for transfers between devices, local(): lax.psum((grad_gain, grad_wexp, grad_kernel, grad_project), ('dp', 'row',...  249 us
    psum x1, blocking collectives, local(): lax.psum((grad_gain, grad_wexp, grad_kernel, grad_project), ('dp', 'row',...  79.1 us
    psum x1, blocking collectives, local(): lax.psum(jnp.sum(grad_gated * act, axis=(2, 3)), ('row', 'col'))  57.2 us
    all_gather x1, blocking collectives, local(): lax.all_gather(jnp.sum(act, axis=(2, 3)), ('row', 'col'))  36.3 us
    ppermute x4, starting transfers between devices, with_halo(): after = lax.ppermute(leading, axis, down)  16.2 us
    unnamed x43, local copies, waits for them, and re-layouts  11.2 us
  transfers between devices with their start and end apart: 10, of which 6 were waited for; matrix products, arithmetic and copies ran while one was open for 2% of the time, Pallas kernels for 0%

profile of v1, /device:TPU:2, one launch (start us, length us, event | category | flops | bytes accessed | tf_op | source)
XLA Modules:
  0.0 526.8 jit_solution(6128884650121812210)
XLA Ops:
  7.2 1.1 fusion.59
  8.4 3.8 fusion.30
  12.2 3.4 collective-permute-start
  15.6 2.5 collective-permute-start.1
  18.1 2.7 collective-permute-done
  20.7 3.1 collective-permute-done.1
  23.9 1.3 collective-permute-start.2
  25.2 1.4 collective-permute-start.3
  26.8 3.5 collective-permute-done.3
  31.3 7.2 %fusion.26 = (f32[768]{0:T(1024)S(1)}, f32[768]{0:T(1024)S(1)}, f32[1,768,8,128]{1,3,2,0:T(8,128)}, f32[768,8,128]{0,2,1:T(8,128)}) fusion(bf16[1,768,10,129]{1,3,2,0:T(8,128)(2,1)S(1)} %get-tuple-element.66, f32[768]{0:T(1024)S(1)} %get-tuple-element.49, bf16[1,768,1,128]{1,3,2,0:T(8,128)(2,1)S(1)} %collective-permute-done.1, ...), kind=kOutput, calls=%fused_computation.48 | convolution fusion | flops 329513472 | bytes 19989504 | tf_op jit(solution)/shard_map/bchw,ec->behw/dot_general | solution.py:69
  38.5 36.3 %all-gather.1 = f32[32,1,768]{2,1,0:T(1,128)S(1)} all-gather(f32[1,1,768]{2,1,0:T(1,128)S(1)} %reshape.166), channel_id=2, replica_groups=mesh['dp'=8,'row'=8,'col'=4] {'row','col'}, dimensions={0}, use_global_device_ids=true | all-gather | bytes 101376 | tf_op jit(solution)/shard_map/all_gather | solution.py:61
  75.4 3.9 fusion.46
  79.3 2.0 convolution_bitcast_fusion.1
  81.3 57.2 %psum.49 = f32[1,768]{1,0:T(1,128)S(1)} all-reduce(f32[1,768]{1,0:T(1,128)S(1)} %reduce_sum.141), channel_id=1, replica_groups=mesh['dp'=8,'row'=8,'col'=4] {'row','col'}, use_global_device_ids=true, to_apply=%region_4.5 | all-reduce | flops 768 | bytes 6144 | tf_op jit(solution)/shard_map/psum | solution.py:73
  138.9 9.3 %fusion.24 = (f32[768]{0:T(1024)S(1)}, f32[768]{0:T(1024)S(1)}, f32[768]{0:T(1024)S(1)}, f32[768]{0:T(1024)S(1)}, f32[768]{0:T(1024)S(1)}, /*index=5*/f32[768]{0...) fusion(bf16[1,768,10,129]{1,3,2,0:T(8,128)(2,1)} %copy-done.2, ...), kind=kLoop, calls=%fused_computation.44 | loop fusion | flops 32236800 | bytes 20874240 | tf_op jit(solution)/shard_map/reduce_sum | solution.py:94
  148.3 2.1 collective-permute-start.4
  150.3 11.0 %collective-permute-start.5 = (bf16[1,768,1,128]{1,3,2,0:T(8,128)(2,1)S(1)}, bf16[1,768,1,128]{1,3,2,0:T(8,128)(2,1)S(1)}, u32[]{:S(2)}, u32[]{:S(2)}) collective-permute-start(bf16[1,768,1,128]{1,3,2,0:T(8,128)(2,1)S(1)} %get-tuple-element.70), channel_id=1, source_target_pairs={{4,0},{8,4},{12,8},{16,12},{20,16},{24,20},{28,24},{5,1},{9,5},{13... | collective-permute-start | bytes 589832 | tf_op jit(solution)/shard_map/ppermute | solution.py:18
  162.1 1.9 collective-permute-done.4
  164.0 1.2 collective-permute-done.5
  165.2 1.3 collective-permute-start.6
  166.5 3.0 collective-permute-start.7
  170.4 1.0 copy.34
  173.6 4.7 fusion.15
  178.4 1.1 copy-done.7
  179.5 1.3 fusion.43
  180.9 2.2 fusion.58
  184.4 79.1 %all-reduce = (f32[192]{0:T(256)}, f32[768,9]{0,1:T(8,128)}) all-reduce(f32[192]{0:T(256)S(1)} %get-tuple-element.40, f32[768,9]{0,1:T(8,128)S(1)} %stack.39), channel_id=1, replica_groups=mesh['dp'=8,'row'=8,'col'=4] {'dp','row','col'}, use_global_device_ids=true, to_apply=%region_7.8 | all-reduce | flops 7104 | bytes 56832 | tf_op jit(solution)/shard_map/psum | solution.py:112
  263.5 249.5 %all-reduce.6.cloned.1.call-done = (f32[192,768]{1,0:T(8,128)}, f32[768,192]{0,1:T(8,128)}) async-done(((f32[192,768]{1,0:T(8,128)}, f32[768,192]{0,1:T(8,128)}), (f32[192,768]{1,0:T(8,128)}, f32[768,192]{0,1:T(8,128)})) %all-reduce.6.cloned.1.call-update) | async-done | bytes 1179664 | tf_op jit(solution)/shard_map/psum | solution.py:112
  512.9 1.9 copy.61
  514.8 1.6 copy.62
  516.4 1.6 copy.63
  518.0 1.9 copy.64
  (78 shorter events, 7.2 us)
Async XLA Ops:
  7.2 24.1 %copy-start = (bf16[768,192]{0,1:T(8,128)(2,1)S(1)}, bf16[768,192]{0,1:T(8,128)(2,1)}, u32[]{:S(2)}) copy-start(bf16[768,192]{0,1:T(8,128)(2,1)} %param.14) | copy-start | bytes 884740
  7.2 256.3 %all-reduce.8.cloned.1.call-start = ((), (), s32[]{:S(2)}) async-start(), calls=%async_computation.1 | async-start | bytes 589824 | tf_op jit(solution)/shard_map/psum | solution.py:111
  8.4 18.3 %copy-start.15 = (f32[768,9]{0,1:T(8,128)S(1)}, f32[768,9]{0,1:T(8,128)}, u32[]{:S(2)}) copy-start(f32[768,9]{0,1:T(8,128)} %param.11) | copy-start | bytes 82948
  12.2 8.5 %collective-permute-start = (bf16[1,768,1,128]{1,3,2,0:T(8,128)(2,1)S(1)}, bf16[1,768,1,128]{1,3,2,0:T(8,128)(2,1)S(1)}, u32[]{:S(2)}, u32[]{:S(2)}) collective-permute-start(bf16[1,768,1,128]{1,3,2,0:T(8,128)(2,1)S(1)} %get-tuple-element.71), channel_id=1, source_target_pairs={{0,4},{4,8},{8,12},{12,16},{16,20},{20,24},{24,28},{1,5},{5,9},{9,... | collective-permute-start | bytes 589832 | tf_op jit(solution)/shard_map/ppermute | solution.py:17
  15.6 8.3 %collective-permute-start.1 = (bf16[1,768,1,128]{1,3,2,0:T(8,128)(2,1)S(1)}, bf16[1,768,1,128]{1,3,2,0:T(8,128)(2,1)S(1)}, u32[]{:S(2)}, u32[]{:S(2)}) collective-permute-start(bf16[1,768,1,128]{1,3,2,0:T(8,128)(2,1)S(1)} %get-tuple-element.72), channel_id=1, source_target_pairs={{4,0},{8,4},{12,8},{16,12},{20,16},{24,20},{28,24},{5,1},{9,5},{13... | collective-permute-start | bytes 589832 | tf_op jit(solution)/shard_map/ppermute | solution.py:18
  20.7 10.5 %copy-start.5 = (bf16[1,768,1,128]{1,3,2,0:T(8,128)(2,1)}, bf16[1,768,1,128]{1,3,2,0:T(8,128)(2,1)S(1)}, u32[]{:S(2)}) copy-start(bf16[1,768,1,128]{1,3,2,0:T(8,128)(2,1)S(1)} %collective-permute-done) | copy-start | bytes 589828
  23.9 7.4 %copy-start.6 = (bf16[1,768,1,128]{1,3,2,0:T(8,128)(2,1)}, bf16[1,768,1,128]{1,3,2,0:T(8,128)(2,1)S(1)}, u32[]{:S(2)}) copy-start(bf16[1,768,1,128]{1,3,2,0:T(8,128)(2,1)S(1)} %collective-permute-done.1) | copy-start | bytes 589828
  23.9 2.8 collective-permute-start.2
  25.2 6.0 %copy-start.12 = (bf16[1,192,8,128]{3,2,1,0:T(8,128)(2,1)S(1)}, bf16[1,192,8,128]{3,2,1,0:T(8,128)(2,1)}, u32[]{:S(2)}) copy-start(bf16[1,192,8,128]{3,2,1,0:T(8,128)(2,1)} %param.15) | copy-start | bytes 1179652
  25.2 5.0 collective-permute-start.3
  31.2 7.3 %copy-start.1 = (bf16[1,768,10,129]{1,3,2,0:T(8,128)(2,1)}, bf16[1,768,10,129]{1,3,2,0:T(8,128)(2,1)S(1)}, u32[]{:S(2)}) copy-start(bf16[1,768,10,129]{1,3,2,0:T(8,128)(2,1)S(1)} %get-tuple-element.65) | copy-start | bytes 5944324
  31.2 7.3 %copy-start.2 = (bf16[1,768,10,129]{1,3,2,0:T(8,128)(2,1)}, bf16[1,768,10,129]{1,3,2,0:T(8,128)(2,1)S(1)}, u32[]{:S(2)}) copy-start(bf16[1,768,10,129]{1,3,2,0:T(8,128)(2,1)S(1)} %get-tuple-element.66) | copy-start | bytes 5944324
  31.2 43.6 %copy-start.11 = (f32[768,48]{0,1:T(8,128)S(1)}, f32[768,48]{0,1:T(8,128)}, u32[]{:S(2)}) copy-start(f32[768,48]{0,1:T(8,128)} %param.12) | copy-start | bytes 442372
  31.3 43.9 %copy-start.10 = (f32[48,768]{1,0:T(8,128)S(1)}, f32[48,768]{1,0:T(8,128)}, u32[]{:S(2)}) copy-start(f32[48,768]{1,0:T(8,128)} %param.13) | copy-start | bytes 442372
  31.3 44.1 %copy-start.8 = (bf16[1,192,8,128]{3,2,1,0:T(8,128)(2,1)S(1)}, bf16[1,192,8,128]{3,2,1,0:T(8,128)(2,1)}, u32[]{:S(2)}) copy-start(bf16[1,192,8,128]{3,2,1,0:T(8,128)(2,1)} %param.8) | copy-start | bytes 1179652
  75.4 3.9 copy-start.4
  148.2 22.2 %copy-start.14 = (bf16[1,192,8,128]{3,1,2,0:T(8,128)(2,1)S(1)}, bf16[1,192,8,128]{3,1,2,0:T(8,128)(2,1)}, u32[]{:S(2)}) copy-start(bf16[1,192,8,128]{3,1,2,0:T(8,128)(2,1)} %fusion.46) | copy-start | bytes 1179652
  148.3 15.7 %collective-permute-start.4 = (bf16[1,768,1,128]{1,3,2,0:T(8,128)(2,1)S(1)}, bf16[1,768,1,128]{1,3,2,0:T(8,128)(2,1)S(1)}, u32[]{:S(2)}, u32[]{:S(2)}) collective-permute-start(bf16[1,768,1,128]{1,3,2,0:T(8,128)(2,1)S(1)} %get-tuple-element.69), channel_id=1, source_target_pairs={{0,4},{4,8},{8,12},{12,16},{16,20},{20,24},{24,28},{1,5},{5,9},{9,... | collective-permute-start | bytes 589832 | tf_op jit(solution)/shard_map/ppermute | solution.py:17
  150.3 14.8 %collective-permute-start.5 = (bf16[1,768,1,128]{1,3,2,0:T(8,128)(2,1)S(1)}, bf16[1,768,1,128]{1,3,2,0:T(8,128)(2,1)S(1)}, u32[]{:S(2)}, u32[]{:S(2)}) collective-permute-start(bf16[1,768,1,128]{1,3,2,0:T(8,128)(2,1)S(1)} %get-tuple-element.70), channel_id=1, source_target_pairs={{4,0},{8,4},{12,8},{16,12},{20,16},{24,20},{28,24},{5,1},{9,5},{13... | collective-permute-start | bytes 589832 | tf_op jit(solution)/shard_map/ppermute | solution.py:18
  165.2 6.5 %collective-permute-start.6 = (bf16[1,768,10,1]{1,3,2,0:T(2,128)(2,1)S(1)}, bf16[1,768,10,1]{1,3,2,0:T(2,128)(2,1)S(1)}, u32[]{:S(2)}, u32[]{:S(2)}) collective-permute-start(bf16[1,768,10,1]{1,3,2,0:T(2,128)(2,1)S(1)} %get-tuple-element.63), channel_id=1, source_target_pairs={{1,0},{2,1},{3,2},{5,4},{6,5},{7,6},{9,8},{10,9},{11,10},{13,12},{... | collective-permute-start | bytes 46088 | tf_op jit(solution)/shard_map/ppermute | solution.py:18
  166.5 5.2 collective-permute-start.7
  171.4 341.5 %all-reduce.6.cloned.1.call-start = ((), (), s32[]{:S(2)}) async-start(), calls=%async_computation | async-start | bytes 2359296 | tf_op jit(solution)/shard_map/psum | solution.py:112
  171.7 1.9 copy-start.3
  173.6 5.9 %copy-start.9 = (bf16[1,192,8,128]{3,2,1,0:T(8,128)(2,1)S(1)}, bf16[1,192,8,128]{3,2,1,0:T(8,128)(2,1)}, u32[]{:S(2)}) copy-start(bf16[1,192,8,128]{3,2,1,0:T(8,128)(2,1)} %param.8) | copy-start | bytes 1179652
  173.6 5.9 %copy-start.16 = (f32[192]{0:T(256)S(1)}, f32[192]{0:T(256)}, u32[]{:S(2)}) copy-start(f32[192]{0:T(256)} %param.9) | copy-start | bytes 2308
  178.4 1.2 copy-start.7
  179.5 1.4 copy-start.17
  179.5 3.6 copy-start.13
Sparse Core Ops, SparseCore 0:
  171.6 75.2 all-reduce.7
  252.9 259.9 all-reduce.5
